TPU v7x, 32 devices: a whole 2x2x4 slice. The times are simulated.
32 devices in a mesh: grp: 1, wide: 8 (over z, y), narrow: 4 (over x, core).
Axes of the slice: x: 2, y: 2, z: 4, core: 2. Of those that a mesh axis runs over, the one named last changes fastest.
Arguments:
- vectors: bfloat16 [512, 2, 3, 16, 512], P('grp', None, None, 'wide', 'narrow'), may hold values from -6 to 6
- links: float32 [3, 2, 3, 3, 16, 512], P('grp', None, None, None, 'wide', 'narrow'), may hold values from -4 to 4
- directions: int32 [3], replicated, may hold values from 0 to 2, each once
- peram: bfloat16 [2, 512, 256], P('grp', 'wide', 'narrow'), may hold values from -0.1875 to 0.1875
Outputs:
- elementals: float32 [3, 2, 512, 512], P('grp', None, 'wide')
- products: float32 [3, 2, 512, 256], P('grp', None, 'wide', 'narrow')
All inputs are finite; a program needn't handle non-finite values.
Results may differ from a plain program's by a relative error of at most 0.004.
Values may be sent and summed in bfloat16 or wider, within the bound.
A program may use at most 64 MiB of HBM per device.

v0:
```python
import math
import jax
import jax.numpy as jnp
from jax import lax
from jax.sharding import PartitionSpec as P

LZ = 16


def from_behind(x, axis, by):
    length = lax.axis_size(axis)
    return lax.ppermute(x, axis, [(i, (i + by) % length) for i in range(length)])


def covariant_product(link_field, shifted):
    link_real = link_field[0][None]
    link_imag = link_field[1][None]
    vec_real = shifted[:, 0][:, None]
    vec_imag = shifted[:, 1][:, None]
    out_real = jnp.sum(link_real * vec_real - link_imag * vec_imag, axis=2)
    out_imag = jnp.sum(link_real * vec_imag + link_imag * vec_real, axis=2)
    return jnp.stack([out_real, out_imag], 1).astype(jnp.bfloat16)


def on_device(vectors, links, directions, peram):
    vec_count = vectors.shape[0]
    plane_count = vectors.shape[3]
    row_length = vectors.shape[4]
    direction_count = directions.shape[0]
    col_count = peram.shape[2]
    wide_count = lax.axis_size("wide")
    narrow_count = lax.axis_size("narrow")
    norm_factor = 1.0 / math.sqrt(12.0 * plane_count * wide_count * row_length * narrow_count)
    next_first = from_behind(vectors[:, :, :, 0:1], "wide", -1)
    along_first = jnp.concatenate([vectors[:, :, :, 1:], next_first], 3)
    next_second = from_behind(vectors[:, :, :, :, 0:LZ], "narrow", -1)
    along_second = jnp.concatenate([vectors[:, :, :, :, LZ:], next_second], 4)
    along_third = jnp.roll(
        vectors.reshape(vec_count, 2, 3, plane_count, row_length // LZ, LZ), -1, axis=5
    ).reshape(vectors.shape)
    rotated = jnp.concatenate([-vectors[:, 1:2], vectors[:, 0:1]], 1)
    left_block = jnp.concatenate(
        [vectors.reshape(vec_count, -1), rotated.reshape(vec_count, -1)], 0
    )
    partials = []
    for slot_index in range(direction_count):
        chosen = directions[slot_index]
        shifted = jnp.where(
            chosen == 0, along_first, jnp.where(chosen == 1, along_second, along_third)
        )
        link_field = jnp.where(chosen == 0, links[0], jnp.where(chosen == 1, links[1], links[2]))
        product = covariant_product(link_field, shifted).reshape(vec_count, -1)
        partials.append(
            lax.dot_general(
                left_block, product, (((1,), (1,)), ((), ())), preferred_element_type=jnp.float32
            )
        )
    halves = jnp.stack(partials).reshape(direction_count, 2, vec_count, vec_count) * norm_factor
    real_part = halves[:, 0]
    imag_part = halves[:, 1]
    local_terms = jnp.stack(
        [real_part - jnp.swapaxes(real_part, 1, 2), imag_part + jnp.swapaxes(imag_part, 1, 2)], 1
    )
    rows_here = vec_count // wide_count
    thin_rows = lax.psum_scatter(local_terms, ("wide", "narrow"), scatter_dimension=2, tiled=True)
    elementals = lax.all_gather(thin_rows, "narrow", axis=2, tiled=True)
    elem_low = elementals.astype(jnp.bfloat16)
    real_rows = elem_low[:, 0]
    imag_rows = elem_low[:, 1]
    piece = lax.all_gather(peram, "wide", axis=1, tiled=True)
    width = piece.shape[1]
    left_part = jnp.concatenate([real_rows, imag_rows], 2).reshape(-1, 2 * width)
    right_part = jnp.concatenate(
        [jnp.concatenate([piece[0], piece[1]], 1), jnp.concatenate([-piece[1], piece[0]], 1)], 0
    )
    summed = jnp.dot(left_part, right_part, preferred_element_type=jnp.float32)
    products = summed.reshape(direction_count, rows_here, 2, col_count).transpose(0, 2, 1, 3)
    return (elementals, products)


def solution(mesh):
    placed = (
        P("grp", None, None, "wide", "narrow"),
        P("grp", None, None, None, "wide", "narrow"),
        P(),
        P("grp", "wide", "narrow"),
    )
    return jax.shard_map(
        on_device,
        mesh=mesh,
        in_specs=placed,
        out_specs=(P("grp", None, "wide", None), P("grp", None, "wide", "narrow")),
        check_vma=False,
    )
```

profile of v0, /device:TPU:0, one launch (start us, length us, event | category | flops | bytes accessed | tf_op | source)
XLA Modules:
  0.0 246.1 jit_solution(10593543814689281994)
XLA Ops:
  7.2 3.6 %copy.27 = bf16[512,2,3,2,128]{0,4,3,2,1:T(8,128)(2,1)S(1)} copy(bf16[512,2,3,2,128]{4,3,2,1,0:T(2,128)(2,1)} %param.4) | data formatting | bytes 3145728 | tf_op args[0]
  12.1 6.0 %collective-permute-start = (bf16[512,2,3,1,128]{0,4,3,2,1:T(8,128)(2,1)}, bf16[512,2,3,1,128]{0,4,3,2,1:T(8,128)(2,1)}, u32[]{:S(2)}, u32[]{:S(2)}) collective-permute-start(bf16[512,2,3,1,128]{0,4,3,2,1:T(8,128)(2,1)} %get-tuple-element.28), channel_id=1, source_target_pairs={{0,28},{4,0},{8,4},{12,8},{16,12},{20,16},{24,20},{28,24},{1,29},{... | collective-permute-start | bytes 2359304 | tf_op jit(solution)/shard_map/ppermute | solution.py:12
  25.2 3.2 %pad_maximum_fusion.2 = bf16[512,2,3,2,128]{4,3,2,1,0:T(2,128)(2,1)} fusion(bf16[512,1,3,2,128]{4,3,2,1,0:T(2,128)(2,1)S(1)} %get-tuple-element.30, bf16[512,1,3,2,128]{4,3,2,1,0:T(2,128)(2,1)S(1)} %get-tuple-element.29), kind=kLoop, calls=%fused_computation.17 | loop fusion | flops 786432 | bytes 3145728 | tf_op jit(solution)/shard_map/concatenate | solution.py:41
  36.6 3.4 %pad_maximum_fusion.1 = bf16[1024,1536]{1,0:T(8,128)(2,1)} fusion(bf16[512,1536]{1,0:T(8,128)(2,1)} %reshape.107, bf16[512,1536]{1,0:T(8,128)(2,1)S(1)} %copy-done.3), kind=kLoop, calls=%fused_computation.9 | loop fusion | flops 6291456 | bytes 6291456 | tf_op jit(solution)/shard_map/concatenate | solution.py:42
  40.7 3.5 %fusion.2 = (bf16[512,2,3,2,128]{0,4,3,2,1:T(8,128)(2,1)S(1)}, bf16[512,2,3,2,128]{0,4,3,2,1:T(8,128)(2,1)}, bf16[512,2,3,2,128]{0,4,3,2,1:T(8,128)(2,1)}) fusion(bf16[512,2,3,2,8,16]{0,5,4,3,2,1:T(8,128)(2,1)S(1)} %copy-done.5, pred[]{:T(512)} %bitcast.2, pred[]{:T(512)} %bitcast.1, bf16[512,2,3,2,16]{0,4,3,2,1:T(8,128)(2,1)S(1)} %collective-permute-done.1, ...), kind=kLoop, calls=%fused_computation.27 | loop fusion | flops 11010048 | bytes 9437190 | tf_op jit(solution)/shard_map/jit(_where)/select_n | solution.py:48
  46.3 1.9 copy.33
  52.9 4.4 %fusion.6 = (f32[512,3,2,128]{0,3,2,1:T(8,128)S(1)}, f32[512,3,2,128]{0,3,2,1:T(8,128)S(1)}, f32[512,3,2,128]{0,3,2,1:T(8,128)}, f32[512,3,2,128]{0,3,2,1:T(8,128)}) fusion(bf16[512,2,3,2,128]{0,4,3,2,1:T(8,128)(2,1)} %get-tuple-element.20, bf16[512,2,3,2,128]{0,4,3,2,1:T(8,128)(2,1)} %get-tuple-element.19), kind=kLoop, calls=%fused_computation.34 | loop fusion | flops 1572864 | bytes 9437184 | tf_op jit(solution)/shard_map/mul | solution.py:20
  57.4 3.1 %copy.35 = f32[512,3,2,128]{3,0,2,1:T(8,128)} copy(f32[512,3,2,128]{0,3,2,1:T(8,128)} %get-tuple-element.48) | data formatting | bytes 3145728 | tf_op jit(solution)/shard_map/mul | solution.py:20
  60.5 3.1 %copy.36 = f32[512,3,2,128]{3,0,2,1:T(8,128)} copy(f32[512,3,2,128]{0,3,2,1:T(8,128)} %get-tuple-element.47) | data formatting | bytes 3145728 | tf_op jit(solution)/shard_map/mul | solution.py:20
  63.6 3.3 %subtract_reduce_fusion.1 = (bf16[512,3,2,128]{3,0,2,1:T(8,128)(2,1)S(1)}, bf16[512,3,2,128]{3,0,2,1:T(8,128)(2,1)S(1)}) fusion(f32[512,3,2,128]{3,0,2,1:T(8,128)} %copy.36, f32[3,3,2,128]{3,2,1,0:T(2,128)S(1)} %copy-done.15, f32[512,3,2,128]{3,0,2,1:T(8,128)} %copy.35, f32[3,3,2,128]{3,2,1,0:T(2,128)S(1)} %copy-done.16), kind=kLoop, calls=%fused_computation.5 | loop fusion | flops 8650752 | bytes 4737024 | tf_op jit(solution)/shard_map/reduce_sum | solution.py:20
  67.0 2.8 %copy.37 = bf16[512,2,3,2,128]{4,3,2,1,0:T(2,128)(2,1)} copy(bf16[512,2,3,2,128]{4,0,3,2,1:T(8,128)(2,1)S(1)} %pad_maximum_fusion.7) | data formatting | bytes 3145728 | tf_op jit(solution)/shard_map/stack | solution.py:22
  69.8 4.9 %reshape.118 = bf16[512,1536,1]{1,0,2:T(8,128)(2,1)} reshape(bf16[512,2,3,2,128]{4,3,2,1,0:T(2,128)(2,1)} %copy.37) | data formatting | bytes 3145728 | tf_op jit(solution)/shard_map/convert_element_type | solution.py:22
  74.7 5.7 %convolution_bitcast_fusion.2 = f32[1,2,512,512]{3,2,1,0:T(8,128)} fusion(bf16[2,512,1536]{2,1,0:T(8,128)(2,1)} %bitcast.135, bf16[512,1536,1]{1,0,2:T(8,128)(2,1)} %reshape.117), kind=kOutput, calls=%fused_computation.16 | convolution fusion | flops 1610612736 | bytes 6815744 | tf_op jit(solution)/shard_map/dot_general | solution.py:54
  80.4 3.2 %convolution_bitcast_fusion.1 = f32[1,2,512,512]{3,2,1,0:T(8,128)} fusion(bf16[2,512,1536]{2,1,0:T(8,128)(2,1)S(1)} %bitcast.137, bf16[512,1536,1]{1,0,2:T(8,128)(2,1)S(1)} %copy-done.11), kind=kOutput, calls=%fused_computation.15 | convolution fusion | flops 1610612736 | bytes 6815744 | tf_op jit(solution)/shard_map/dot_general | solution.py:54
  86.9 2.8 %subtract_reduce_fusion = (bf16[512,3,2,128]{3,0,2,1:T(8,128)(2,1)S(1)}, bf16[512,3,2,128]{3,0,2,1:T(8,128)(2,1)S(1)}) fusion(f32[512,3,2,128]{3,0,2,1:T(8,128)} %copy.39, f32[3,3,2,128]{3,2,1,0:T(2,128)S(1)} %copy-done.14, f32[512,3,2,128]{3,0,2,1:T(8,128)S(1)} %copy-done.4, f32[3,3,2,128]{3,2,1,0:T(2,128)S(1)} %get-tuple-element.42), kind=kLoop, calls=%fused_computation.3 | loop fusion | flops 8650752 | bytes 4737024 | tf_op jit(solution)/shard_map/reduce_sum | solution.py:20
  92.2 3.9 %convolution_bitcast_fusion = f32[1,2,512,512]{3,2,1,0:T(8,128)S(1)} fusion(bf16[2,512,1536]{2,1,0:T(8,128)(2,1)} %bitcast.136, bf16[512,1536,1]{1,0,2:T(8,128)(2,1)S(1)} %reshape.119), kind=kOutput, calls=%fused_computation.14 | convolution fusion | flops 1610612736 | bytes 6815744 | tf_op jit(solution)/shard_map/dot_general | solution.py:54
  97.4 3.7 %fusion.15 = (f32[3,1,512,512]{3,2,1,0:T(8,128)}, f32[3,512,512]{2,1,0:T(8,128)}) fusion(f32[3,2,512,512]{3,2,1,0:T(8,128)S(1)} %maximum_multiply_fusion), kind=kLoop, calls=%fused_computation.69 | loop fusion | bytes 12582912 | tf_op jit(solution)/shard_map/slice | solution.py:59
  101.9 2.4 copy.43
  104.3 3.5 %copy.47 = f32[3,1,512,512]{2,3,0,1:T(8,128)} copy(f32[3,1,512,512]{3,2,1,0:T(8,128)} %get-tuple-element.16) | data formatting | bytes 6291456
  107.8 5.3 %fusion = (f32[3,1,512,512]{3,2,0,1:T(8,128)S(1)}, f32[3,1,512,512]{3,2,0,1:T(8,128)S(1)}) fusion(f32[3,1,512,512]{2,3,0,1:T(8,128)} %copy.47, f32[3,2,512,512]{3,2,1,0:T(8,128)} %copy-done, f32[3,512,512]{1,2,0:T(8,128)S(1)} %copy.43), kind=kLoop, calls=%fused_computation.11 | loop fusion | flops 1572864 | bytes 18874368 | tf_op jit(solution)/shard_map/stack | solution.py:61
  113.2 3.4 %pad_maximum_fusion = f32[3,2,512,512]{3,2,0,1:T(8,128)} fusion(f32[3,1,512,512]{3,2,0,1:T(8,128)S(1)} %get-tuple-element.15, f32[3,1,512,512]{3,2,0,1:T(8,128)S(1)} %get-tuple-element.14), kind=kLoop, calls=%fused_computation.1 | loop fusion | flops 1572864 | bytes 12582912 | tf_op jit(solution)/shard_map/stack | solution.py:61
  117.3 30.8 %all_gather.7 = bf16[2,512,64]{2,1,0:T(8,128)(2,1)S(1)} all-gather(bf16[2,64,64]{2,1,0:T(8,128)(2,1)S(1)} %copy-done.19), channel_id=1, replica_groups=mesh['grp'=1,'wide'=8,'narrow'=4] {'wide'}, dimensions={1}, use_global_device_ids=true | all-gather | bytes 147456 | tf_op jit(solution)/shard_map/all_gather | solution.py:70
  148.4 79.9 %reduce-scatter.2.cloned.1.call-done = f32[3,2,16,512]{3,2,0,1:T(8,128)} async-done(((f32[3,2,512,512]{3,2,0,1:T(8,128)}), f32[3,2,16,512]{3,2,0,1:T(8,128)}) %reduce-scatter.2.cloned.1.call-update) | async-done | bytes 196624 | tf_op jit(solution)/shard_map/reduce_scatter | solution.py:65
  228.4 8.9 %all_gather.6 = f32[3,2,64,512]{3,2,0,1:T(8,128)S(1)} all-gather(f32[3,2,16,512]{3,2,0,1:T(8,128)} %reduce-scatter.2.cloned.1.call-done), channel_id=1, replica_groups=mesh['grp'=1,'wide'=8,'narrow'=4] {'narrow'}, dimensions={2}, use_global_device_ids=true | all-gather | bytes 983040 | tf_op jit(solution)/shard_map/all_gather | solution.py:66
  (81 shorter events, 31.4 us)
Async XLA Ops:
  7.2 221.2 %reduce-scatter.2.cloned.1.call-start = ((), (), s32[]{:S(2)}) async-start(), calls=%async_computation.1 | async-start | bytes 6488064 | tf_op jit(solution)/shard_map/reduce_scatter | solution.py:65
  12.1 7.7 %copy-start.20 = (s32[3]{0:T(128)S(1)}, s32[3]{0:T(128)}, u32[]{:S(2)}) copy-start(s32[3]{0:T(128)} %param.6) | copy-start | bytes 40
  12.1 11.9 %copy-start.1 = (bf16[512,2,3,2,128]{4,3,2,1,0:T(2,128)(2,1)S(1)}, bf16[512,2,3,2,128]{4,3,2,1,0:T(2,128)(2,1)}, u32[]{:S(2)}) copy-start(bf16[512,2,3,2,128]{4,3,2,1,0:T(2,128)(2,1)} %param.4) | copy-start | bytes 4718596
  12.1 28.5 %collective-permute-start = (bf16[512,2,3,1,128]{0,4,3,2,1:T(8,128)(2,1)}, bf16[512,2,3,1,128]{0,4,3,2,1:T(8,128)(2,1)}, u32[]{:S(2)}, u32[]{:S(2)}) collective-permute-start(bf16[512,2,3,1,128]{0,4,3,2,1:T(8,128)(2,1)} %get-tuple-element.28), channel_id=1, source_target_pairs={{0,28},{4,0},{8,4},{12,8},{16,12},{20,16},{24,20},{28,24},{1,29},{... | collective-permute-start | bytes 2359304 | tf_op jit(solution)/shard_map/ppermute | solution.py:12
  18.2 22.5 %collective-permute-start.1 = (bf16[512,2,3,2,16]{0,4,3,2,1:T(8,128)(2,1)S(1)}, bf16[512,2,3,2,16]{0,4,3,2,1:T(8,128)(2,1)S(1)}, u32[]{:S(2)}, u32[]{:S(2)}) collective-permute-start(bf16[512,2,3,2,16]{0,4,3,2,1:T(8,128)(2,1)S(1)} %slice.148), channel_id=1, source_target_pairs={{0,3},{1,0},{2,1},{3,2},{4,7},{5,4},{6,5},{7,6},{8,11},{9,8},{10,9... | collective-permute-start | bytes 589832 | tf_op jit(solution)/shard_map/ppermute | solution.py:12
  25.2 3.2 %copy-start.13 = (f32[3,2,3,3,2,128]{5,4,3,2,1,0:T(2,128)S(1)}, f32[3,2,3,3,2,128]{5,4,3,2,1,0:T(2,128)}, u32[]{:S(2)}) copy-start(f32[3,2,3,3,2,128]{5,4,3,2,1,0:T(2,128)} %param.5) | copy-start | bytes 165892
  31.9 1.8 copy-start.2
  33.7 2.9 %copy-start.3 = (bf16[512,1536]{1,0:T(8,128)(2,1)S(1)}, bf16[512,1536]{1,0:T(8,128)(2,1)}, u32[]{:S(2)}) copy-start(bf16[512,1536]{1,0:T(8,128)(2,1)} %reshape.106) | copy-start | bytes 4718596
  36.6 3.4 %copy-start.12 = (f32[1,2,3,3,2,128]{5,4,3,2,1,0:T(2,128)S(1)}, f32[1,2,3,3,2,128]{5,4,3,2,1,0:T(2,128)}, u32[]{:S(2)}) copy-start(f32[1,2,3,3,2,128]{5,4,3,2,1,0:T(2,128)} %get-tuple-element.35) | copy-start | bytes 55300
  36.6 4.1 %copy-start.5 = (bf16[512,2,3,2,8,16]{0,5,4,3,2,1:T(8,128)(2,1)S(1)}, bf16[512,2,3,2,8,16]{0,5,4,3,2,1:T(8,128)(2,1)}, u32[]{:S(2)}) copy-start(bf16[512,2,3,2,8,16]{0,5,4,3,2,1:T(8,128)(2,1)} %pad_maximum_fusion.5) | copy-start | bytes 4718596
  36.6 4.1 %copy-start.6 = (bf16[512,2,3,2,112]{0,4,3,2,1:T(8,128)(2,1)S(1)}, bf16[512,2,3,2,112]{0,4,3,2,1:T(8,128)(2,1)}, u32[]{:S(2)}) copy-start(bf16[512,2,3,2,112]{0,4,3,2,1:T(8,128)(2,1)} %slice.147) | copy-start | bytes 4128772
  36.6 4.1 %copy-start.8 = (bf16[512,2,3,1,128]{0,4,3,2,1:T(8,128)(2,1)S(1)}, bf16[512,2,3,1,128]{0,4,3,2,1:T(8,128)(2,1)}, u32[]{:S(2)}) copy-start(bf16[512,2,3,1,128]{0,4,3,2,1:T(8,128)(2,1)} %get-tuple-element.27) | copy-start | bytes 2359300
  46.3 1.9 copy-start.17
  46.3 1.9 copy-start.18
  60.5 3.1 %copy-start.15 = (f32[3,3,2,128]{3,2,1,0:T(2,128)S(1)}, f32[3,3,2,128]{3,2,1,0:T(2,128)}, u32[]{:S(2)}) copy-start(f32[3,3,2,128]{3,2,1,0:T(2,128)} %get-tuple-element.49) | copy-start | bytes 27652
  60.5 3.1 %copy-start.16 = (f32[3,3,2,128]{3,2,1,0:T(2,128)S(1)}, f32[3,3,2,128]{3,2,1,0:T(2,128)}, u32[]{:S(2)}) copy-start(f32[3,3,2,128]{3,2,1,0:T(2,128)} %get-tuple-element.50) | copy-start | bytes 27652
  74.7 5.7 %copy-start.7 = (bf16[1024,1536]{1,0:T(8,128)(2,1)S(1)}, bf16[1024,1536]{1,0:T(8,128)(2,1)}, u32[]{:S(2)}) copy-start(bf16[1024,1536]{1,0:T(8,128)(2,1)} %pad_maximum_fusion.1) | copy-start | bytes 9437188
  74.7 5.7 %copy-start.11 = (bf16[512,1536,1]{1,0,2:T(8,128)(2,1)S(1)}, bf16[512,1536,1]{1,0,2:T(8,128)(2,1)}, u32[]{:S(2)}) copy-start(bf16[512,1536,1]{1,0,2:T(8,128)(2,1)} %reshape.118) | copy-start | bytes 4718596
  85.2 1.7 copy-start.4
  85.2 1.7 copy-start.14
  92.2 3.9 %copy-start.9 = (f32[1,2,512,512]{3,2,1,0:T(8,128)S(1)}, f32[1,2,512,512]{3,2,1,0:T(8,128)}, u32[]{:S(2)}) copy-start(f32[1,2,512,512]{3,2,1,0:T(8,128)} %convolution_bitcast_fusion.2) | copy-start | bytes 6291460
  92.2 3.9 %copy-start.10 = (f32[1,2,512,512]{3,2,1,0:T(8,128)S(1)}, f32[1,2,512,512]{3,2,1,0:T(8,128)}, u32[]{:S(2)}) copy-start(f32[1,2,512,512]{3,2,1,0:T(8,128)} %convolution_bitcast_fusion.1) | copy-start | bytes 6291460
  97.4 4.6 %copy-start = (f32[3,2,512,512]{3,2,1,0:T(8,128)}, f32[3,2,512,512]{3,2,1,0:T(8,128)S(1)}, u32[]{:S(2)}) copy-start(f32[3,2,512,512]{3,2,1,0:T(8,128)S(1)} %maximum_multiply_fusion) | copy-start | bytes 18874372
  116.5 0.8 copy-start.19
Sparse Core Ops, SparseCore 0:
  116.7 111.6 reduce-scatter.1
where the time goes:
time: 247 us; the launch traced here: 246 us
  waiting for transfers between devices  79.9 us (32%)
  local copies, waits for them, and re-layouts  50.1 us (20%)
  blocking collectives  39.7 us (16%)
  other arithmetic  37.9 us (15%)
  between operations  18 us (7%)
  matrix products  13.7 us (6%)
  starting transfers between devices  6.77 us (3%)
    reduce_scatter x1, waiting for transfers between devices, on_device(): lax.psum_scatter(local_terms, ('wide', 'narrow'), scatter_dimension=2, ti...  79.9 us
    all_gather x1, blocking collectives, on_device(): piece = lax.all_gather(peram, 'wide', axis=1, tiled=True)  30.8 us
    mul x8, local copies, waits for them, and re-layouts, covariant_product(): out_real = jnp.sum(link_real * vec_real - link_imag * vec_imag, axis=2)  13.8 us
    dot_general x3, matrix products, on_device(): lax.dot_general(left_block, product, (((1,), (1,)), ((), ())), preferred_...  12.7 us
    unnamed x45, local copies, waits for them, and re-layouts  9.99 us
    all_gather x1, blocking collectives, on_device(): elementals = lax.all_gather(thin_rows, 'narrow', axis=2, tiled=True)  8.85 us
    another operation x2, other arithmetic, on_device(): jnp.stack([real_part - jnp.swapaxes(real_part, 1, 2), imag_part + jnp.swa...  8.68 us
    reduce_sum x3, other arithmetic, covariant_product(): out_real = jnp.sum(link_real * vec_real - link_imag * vec_imag, axis=2)  7.61 us
  transfers between devices with their start and end apart: 3, of which 1 were waited for; matrix products, arithmetic and copies ran while one was open for 7% of the time, Pallas kernels for 0%

commit v1 on v0

--- a/solution.py
+++ b/solution.py
@@ -3,8 +3,24 @@
 import jax.numpy as jnp
 from jax import lax
 from jax.sharding import PartitionSpec as P
+from jax.lax import axis_index, axis_size, ppermute
 
 LZ = 16
+
+
+def views_update(u, dim_at):
+    peer_axis = "wide"
+    n_dev_all = axis_size(peer_axis)
+    block_last = sorted(((h, (h + 1) % n_dev_all) for h in range(n_dev_all)))
+    local_out = u
+    so_far_all = [local_out]
+    for src_i in range(1, n_dev_all):
+        local_out = ppermute(local_out, peer_axis, block_last)
+        so_far_all.insert(0, local_out)
+    tile_out = jnp.concatenate(so_far_all, axis=dim_at)
+    piece_now = axis_index(peer_axis)
+    plain = piece_now + 1
+    return jnp.roll(tile_out, plain * u.shape[dim_at], dim_at)
 
 
 def from_behind(x, axis, by):
@@ -67,7 +83,7 @@
     elem_low = elementals.astype(jnp.bfloat16)
     real_rows = elem_low[:, 0]
     imag_rows = elem_low[:, 1]
-    piece = lax.all_gather(peram, "wide", axis=1, tiled=True)
+    piece = views_update(peram, 1)
     width = piece.shape[1]
     left_part = jnp.concatenate([real_rows, imag_rows], 2).reshape(-1, 2 * width)
     right_part = jnp.concatenate(

time: 247 us -> 247 us (level)
  waiting for transfers between devices: 79.9 us -> 111 us
  blocking collectives: 39.7 us -> 8.66 us
    ppermute x0 -> x7, waiting for transfers between devices: none -> 46.4 us  [views_update(): local_out = ppermute(local_out, peer_axis, block_last)]
    all_gather x1 -> x0, blocking collectives: 30.8 us -> none  [on_device(): piece = lax.all_gather(peram, 'wide', axis=1, tiled=True)]
    reduce_scatter x1, waiting for transfers between devices: 79.9 us -> 64.1 us  [on_device(): lax.psum_scatter(local_terms, ('wide', 'narrow'), scatter_dimension=2, ti...]
    unnamed x45 -> x60, local copies, waits for them, and re-layouts: 9.99 us -> 10.1 us
  transfers between devices with their start and end apart: 3 -> 10, of which waited for: 1 -> 8; matrix products, arithmetic and copies ran while one was open for 7% -> 7% of each run, Pallas kernels for 0% -> 0%
where the time goes in v1:
time: 247 us; the launch traced here: 246 us
  waiting for transfers between devices  111 us (45%)
  local copies, waits for them, and re-layouts  50.5 us (20%)
  other arithmetic  37.9 us (15%)
  between operations  18.3 us (7%)
  matrix products  13.7 us (6%)
  blocking collectives  8.66 us (4%)
  starting transfers between devices  6.79 us (3%)
    reduce_scatter x1, waiting for transfers between devices, on_device(): lax.psum_scatter(local_terms, ('wide', 'narrow'), scatter_dimension=2, ti...  64.1 us
    ppermute x7, waiting for transfers between devices, views_update(): local_out = ppermute(local_out, peer_axis, block_last)  46.4 us
    mul x8, local copies, waits for them, and re-layouts, covariant_product(): out_real = jnp.sum(link_real * vec_real - link_imag * vec_imag, axis=2)  13.8 us
    dot_general x3, matrix products, on_device(): lax.dot_general(left_block, product, (((1,), (1,)), ((), ())), preferred_...  12.7 us
    unnamed x60, local copies, waits for them, and re-layouts  10.1 us
    another operation x2, other arithmetic, on_device(): jnp.stack([real_part - jnp.swapaxes(real_part, 1, 2), imag_part + jnp.swa...  8.67 us
    all_gather x1, blocking collectives, on_device(): elementals = lax.all_gather(thin_rows, 'narrow', axis=2, tiled=True)  8.66 us
    reduce_sum x3, other arithmetic, covariant_product(): out_real = jnp.sum(link_real * vec_real - link_imag * vec_imag, axis=2)  7.61 us
  transfers between devices with their start and end apart: 10, of which 8 were waited for; matrix products, arithmetic and copies ran while one was open for 7% of the time, Pallas kernels for 0%

profile of v1, /device:TPU:0, one launch (start us, length us, event | category | flops | bytes accessed | tf_op | source)
XLA Modules:
  0.0 246.4 jit_solution(9213583524451780527)
XLA Ops:
  7.2 3.6 %copy.27 = bf16[512,2,3,2,128]{0,4,3,2,1:T(8,128)(2,1)S(1)} copy(bf16[512,2,3,2,128]{4,3,2,1,0:T(2,128)(2,1)} %param.4) | data formatting | bytes 3145728 | tf_op args[0]
  12.1 6.0 %collective-permute-start = (bf16[512,2,3,1,128]{0,4,3,2,1:T(8,128)(2,1)}, bf16[512,2,3,1,128]{0,4,3,2,1:T(8,128)(2,1)}, u32[]{:S(2)}, u32[]{:S(2)}) collective-permute-start(bf16[512,2,3,1,128]{0,4,3,2,1:T(8,128)(2,1)} %get-tuple-element.30), channel_id=1, source_target_pairs={{0,28},{4,0},{8,4},{12,8},{16,12},{20,16},{24,20},{28,24},{1,29},{... | collective-permute-start | bytes 2359304 | tf_op jit(solution)/shard_map/ppermute | solution.py:28
  25.5 3.2 %pad_maximum_fusion.2 = bf16[512,2,3,2,128]{4,3,2,1,0:T(2,128)(2,1)} fusion(bf16[512,1,3,2,128]{4,3,2,1,0:T(2,128)(2,1)S(1)} %get-tuple-element.32, bf16[512,1,3,2,128]{4,3,2,1,0:T(2,128)(2,1)S(1)} %get-tuple-element.31), kind=kLoop, calls=%fused_computation.17 | loop fusion | flops 786432 | bytes 3145728 | tf_op jit(solution)/shard_map/concatenate | solution.py:57
  37.0 3.4 %pad_maximum_fusion.1 = bf16[1024,1536]{1,0:T(8,128)(2,1)} fusion(bf16[512,1536]{1,0:T(8,128)(2,1)} %reshape.107, bf16[512,1536]{1,0:T(8,128)(2,1)S(1)} %copy-done.3), kind=kLoop, calls=%fused_computation.9 | loop fusion | flops 6291456 | bytes 6291456 | tf_op jit(solution)/shard_map/concatenate | solution.py:58
  41.1 3.5 %fusion.2 = (bf16[512,2,3,2,128]{0,4,3,2,1:T(8,128)(2,1)S(1)}, bf16[512,2,3,2,128]{0,4,3,2,1:T(8,128)(2,1)}, bf16[512,2,3,2,128]{0,4,3,2,1:T(8,128)(2,1)}) fusion(bf16[512,2,3,2,8,16]{0,5,4,3,2,1:T(8,128)(2,1)S(1)} %copy-done.5, pred[]{:T(512)} %bitcast.2, pred[]{:T(512)} %bitcast.1, bf16[512,2,3,2,16]{0,4,3,2,1:T(8,128)(2,1)S(1)} %collective-permute-done.1, ...), kind=kLoop, calls=%fused_computation.27 | loop fusion | flops 11010048 | bytes 9437190 | tf_op jit(solution)/shard_map/jit(_where)/select_n | solution.py:64
  53.4 4.4 %fusion.6 = (f32[512,3,2,128]{0,3,2,1:T(8,128)S(1)}, f32[512,3,2,128]{0,3,2,1:T(8,128)S(1)}, f32[512,3,2,128]{0,3,2,1:T(8,128)}, f32[512,3,2,128]{0,3,2,1:T(8,128)}) fusion(bf16[512,2,3,2,128]{0,4,3,2,1:T(8,128)(2,1)} %get-tuple-element.22, bf16[512,2,3,2,128]{0,4,3,2,1:T(8,128)(2,1)} %get-tuple-element.21), kind=kLoop, calls=%fused_computation.34 | loop fusion | flops 1572864 | bytes 9437184 | tf_op jit(solution)/shard_map/mul | solution.py:36
  64.0 3.3 %subtract_reduce_fusion.1 = (bf16[512,3,2,128]{3,0,2,1:T(8,128)(2,1)S(1)}, bf16[512,3,2,128]{3,0,2,1:T(8,128)(2,1)S(1)}) fusion(f32[512,3,2,128]{3,0,2,1:T(8,128)} %copy.36, f32[3,3,2,128]{3,2,1,0:T(2,128)S(1)} %copy-done.16, f32[512,3,2,128]{3,0,2,1:T(8,128)} %copy.35, f32[3,3,2,128]{3,2,1,0:T(2,128)S(1)} %copy-done.17), kind=kLoop, calls=%fused_computation.5 | loop fusion | flops 8650752 | bytes 4737024 | tf_op jit(solution)/shard_map/reduce_sum | solution.py:36
  70.3 4.9 %reshape.118 = bf16[512,1536,1]{1,0,2:T(8,128)(2,1)} reshape(bf16[512,2,3,2,128]{4,3,2,1,0:T(2,128)(2,1)} %copy.37) | data formatting | bytes 3145728 | tf_op jit(solution)/shard_map/convert_element_type | solution.py:38
  75.2 5.7 %convolution_bitcast_fusion.2 = f32[1,2,512,512]{3,2,1,0:T(8,128)} fusion(bf16[2,512,1536]{2,1,0:T(8,128)(2,1)} %bitcast.134, bf16[512,1536,1]{1,0,2:T(8,128)(2,1)} %reshape.117), kind=kOutput, calls=%fused_computation.16 | convolution fusion | flops 1610612736 | bytes 6815744 | tf_op jit(solution)/shard_map/dot_general | solution.py:70
  80.9 3.2 %convolution_bitcast_fusion.1 = f32[1,2,512,512]{3,2,1,0:T(8,128)} fusion(bf16[2,512,1536]{2,1,0:T(8,128)(2,1)S(1)} %bitcast.136, bf16[512,1536,1]{1,0,2:T(8,128)(2,1)S(1)} %copy-done.11), kind=kOutput, calls=%fused_computation.15 | convolution fusion | flops 1610612736 | bytes 6815744 | tf_op jit(solution)/shard_map/dot_general | solution.py:70
  92.7 3.9 %convolution_bitcast_fusion = f32[1,2,512,512]{3,2,1,0:T(8,128)S(1)} fusion(bf16[2,512,1536]{2,1,0:T(8,128)(2,1)} %bitcast.135, bf16[512,1536,1]{1,0,2:T(8,128)(2,1)S(1)} %reshape.119), kind=kOutput, calls=%fused_computation.14 | convolution fusion | flops 1610612736 | bytes 6815744 | tf_op jit(solution)/shard_map/dot_general | solution.py:70
  97.8 3.8 %fusion.15 = (f32[3,1,512,512]{3,2,1,0:T(8,128)}, f32[3,512,512]{2,1,0:T(8,128)}) fusion(f32[3,2,512,512]{3,2,1,0:T(8,128)S(1)} %maximum_multiply_fusion), kind=kLoop, calls=%fused_computation.85 | loop fusion | bytes 12582912 | tf_op jit(solution)/shard_map/slice | solution.py:75
  104.8 3.5 %copy.47 = f32[3,1,512,512]{2,3,0,1:T(8,128)} copy(f32[3,1,512,512]{3,2,1,0:T(8,128)} %get-tuple-element.18) | data formatting | bytes 6291456
  108.3 5.3 %fusion = (f32[3,1,512,512]{3,2,0,1:T(8,128)S(1)}, f32[3,1,512,512]{3,2,0,1:T(8,128)S(1)}) fusion(f32[3,1,512,512]{2,3,0,1:T(8,128)} %copy.47, f32[3,2,512,512]{3,2,1,0:T(8,128)} %copy-done, f32[3,512,512]{1,2,0:T(8,128)S(1)} %copy.43), kind=kLoop, calls=%fused_computation.11 | loop fusion | flops 1572864 | bytes 18874368 | tf_op jit(solution)/shard_map/stack | solution.py:77
  113.6 3.4 %pad_maximum_fusion = f32[3,2,512,512]{3,2,0,1:T(8,128)} fusion(f32[3,1,512,512]{3,2,0,1:T(8,128)S(1)} %get-tuple-element.17, f32[3,1,512,512]{3,2,0,1:T(8,128)S(1)} %get-tuple-element.16), kind=kLoop, calls=%fused_computation.1 | loop fusion | flops 1572864 | bytes 12582912 | tf_op jit(solution)/shard_map/stack | solution.py:77
  117.7 6.6 %collective-permute-done.2 = bf16[2,64,64]{2,1,0:T(8,128)(2,1)S(1)} collective-permute-done((bf16[2,64,64]{2,1,0:T(8,128)(2,1)S(1)}, bf16[2,64,64]{2,1,0:T(8,128)(2,1)S(1)}, u32[]{:S(2)}, u32[]{:S(2)}) %collective-permute-start.2) | collective-permute-done | bytes 16416 | tf_op jit(solution)/shard_map/ppermute | solution.py:18
  124.3 6.6 %collective-permute-done.3 = bf16[2,64,64]{2,1,0:T(8,128)(2,1)S(1)} collective-permute-done((bf16[2,64,64]{2,1,0:T(8,128)(2,1)S(1)}, bf16[2,64,64]{2,1,0:T(8,128)(2,1)S(1)}, u32[]{:S(2)}, u32[]{:S(2)}) %collective-permute-start.3) | collective-permute-done | bytes 16416 | tf_op jit(solution)/shard_map/ppermute | solution.py:18
  131.0 6.6 %collective-permute-done.4 = bf16[2,64,64]{2,1,0:T(8,128)(2,1)S(1)} collective-permute-done((bf16[2,64,64]{2,1,0:T(8,128)(2,1)S(1)}, bf16[2,64,64]{2,1,0:T(8,128)(2,1)S(1)}, u32[]{:S(2)}, u32[]{:S(2)}) %collective-permute-start.4) | collective-permute-done | bytes 16416 | tf_op jit(solution)/shard_map/ppermute | solution.py:18
  137.6 6.6 %collective-permute-done.5 = bf16[2,64,64]{2,1,0:T(8,128)(2,1)S(1)} collective-permute-done((bf16[2,64,64]{2,1,0:T(8,128)(2,1)S(1)}, bf16[2,64,64]{2,1,0:T(8,128)(2,1)S(1)}, u32[]{:S(2)}, u32[]{:S(2)}) %collective-permute-start.5) | collective-permute-done | bytes 16416 | tf_op jit(solution)/shard_map/ppermute | solution.py:18
  144.2 6.7 %collective-permute-done.6 = bf16[2,64,64]{2,1,0:T(8,128)(2,1)S(1)} collective-permute-done((bf16[2,64,64]{2,1,0:T(8,128)(2,1)S(1)}, bf16[2,64,64]{2,1,0:T(8,128)(2,1)S(1)}, u32[]{:S(2)}, u32[]{:S(2)}) %collective-permute-start.6) | collective-permute-done | bytes 16416 | tf_op jit(solution)/shard_map/ppermute | solution.py:18
  150.9 6.6 %collective-permute-done.7 = bf16[2,64,64]{2,1,0:T(8,128)(2,1)S(1)} collective-permute-done((bf16[2,64,64]{2,1,0:T(8,128)(2,1)S(1)}, bf16[2,64,64]{2,1,0:T(8,128)(2,1)S(1)}, u32[]{:S(2)}, u32[]{:S(2)}) %collective-permute-start.7) | collective-permute-done | bytes 16416 | tf_op jit(solution)/shard_map/ppermute | solution.py:18
  157.5 6.6 %collective-permute-done.8 = bf16[2,64,64]{2,1,0:T(8,128)(2,1)S(1)} collective-permute-done((bf16[2,64,64]{2,1,0:T(8,128)(2,1)S(1)}, bf16[2,64,64]{2,1,0:T(8,128)(2,1)S(1)}, u32[]{:S(2)}, u32[]{:S(2)}) %collective-permute-start.8) | collective-permute-done | bytes 16416 | tf_op jit(solution)/shard_map/ppermute | solution.py:18
  164.7 64.1 %reduce-scatter.2.cloned.1.call-done = f32[3,2,16,512]{3,2,0,1:T(8,128)} async-done(((f32[3,2,512,512]{3,2,0,1:T(8,128)}), f32[3,2,16,512]{3,2,0,1:T(8,128)}) %reduce-scatter.2.cloned.1.call-update) | async-done | bytes 196624 | tf_op jit(solution)/shard_map/reduce_scatter | solution.py:81
  228.9 8.7 %all_gather.3 = f32[3,2,64,512]{3,2,0,1:T(8,128)S(1)} all-gather(f32[3,2,16,512]{3,2,0,1:T(8,128)} %reduce-scatter.2.cloned.1.call-done), channel_id=1, replica_groups=mesh['grp'=1,'wide'=8,'narrow'=4] {'narrow'}, dimensions={2}, use_global_device_ids=true | all-gather | bytes 983040 | tf_op jit(solution)/shard_map/all_gather | solution.py:82
  (110 shorter events, 47.8 us)
Async XLA Ops:
  7.2 221.7 %reduce-scatter.2.cloned.1.call-start = ((), (), s32[]{:S(2)}) async-start(), calls=%async_computation.1 | async-start | bytes 6488064 | tf_op jit(solution)/shard_map/reduce_scatter | solution.py:81
  12.1 7.7 %copy-start.20 = (s32[3]{0:T(128)S(1)}, s32[3]{0:T(128)}, u32[]{:S(2)}) copy-start(s32[3]{0:T(128)} %param.6) | copy-start | bytes 40
  12.1 12.3 %copy-start.1 = (bf16[512,2,3,2,128]{4,3,2,1,0:T(2,128)(2,1)S(1)}, bf16[512,2,3,2,128]{4,3,2,1,0:T(2,128)(2,1)}, u32[]{:S(2)}) copy-start(bf16[512,2,3,2,128]{4,3,2,1,0:T(2,128)(2,1)} %param.4) | copy-start | bytes 4718596
  12.1 28.9 %collective-permute-start = (bf16[512,2,3,1,128]{0,4,3,2,1:T(8,128)(2,1)}, bf16[512,2,3,1,128]{0,4,3,2,1:T(8,128)(2,1)}, u32[]{:S(2)}, u32[]{:S(2)}) collective-permute-start(bf16[512,2,3,1,128]{0,4,3,2,1:T(8,128)(2,1)} %get-tuple-element.30), channel_id=1, source_target_pairs={{0,28},{4,0},{8,4},{12,8},{16,12},{20,16},{24,20},{28,24},{1,29},{... | collective-permute-start | bytes 2359304 | tf_op jit(solution)/shard_map/ppermute | solution.py:28
  18.2 22.8 %collective-permute-start.1 = (bf16[512,2,3,2,16]{0,4,3,2,1:T(8,128)(2,1)S(1)}, bf16[512,2,3,2,16]{0,4,3,2,1:T(8,128)(2,1)S(1)}, u32[]{:S(2)}, u32[]{:S(2)}) collective-permute-start(bf16[512,2,3,2,16]{0,4,3,2,1:T(8,128)(2,1)S(1)} %slice.148), channel_id=1, source_target_pairs={{0,3},{1,0},{2,1},{3,2},{4,7},{5,4},{6,5},{7,6},{8,11},{9,8},{10,9... | collective-permute-start | bytes 589832 | tf_op jit(solution)/shard_map/ppermute | solution.py:28
  25.5 3.3 %copy-start.14 = (f32[3,2,3,3,2,128]{5,4,3,2,1,0:T(2,128)S(1)}, f32[3,2,3,3,2,128]{5,4,3,2,1,0:T(2,128)}, u32[]{:S(2)}) copy-start(f32[3,2,3,3,2,128]{5,4,3,2,1,0:T(2,128)} %param.5) | copy-start | bytes 165892
  37.0 3.4 %copy-start.13 = (f32[1,2,3,3,2,128]{5,4,3,2,1,0:T(2,128)S(1)}, f32[1,2,3,3,2,128]{5,4,3,2,1,0:T(2,128)}, u32[]{:S(2)}) copy-start(f32[1,2,3,3,2,128]{5,4,3,2,1,0:T(2,128)} %get-tuple-element.35) | copy-start | bytes 55300
  37.0 4.0 %copy-start.5 = (bf16[512,2,3,2,8,16]{0,5,4,3,2,1:T(8,128)(2,1)S(1)}, bf16[512,2,3,2,8,16]{0,5,4,3,2,1:T(8,128)(2,1)}, u32[]{:S(2)}) copy-start(bf16[512,2,3,2,8,16]{0,5,4,3,2,1:T(8,128)(2,1)} %pad_maximum_fusion.5) | copy-start | bytes 4718596
  37.0 4.0 %copy-start.6 = (bf16[512,2,3,2,112]{0,4,3,2,1:T(8,128)(2,1)S(1)}, bf16[512,2,3,2,112]{0,4,3,2,1:T(8,128)(2,1)}, u32[]{:S(2)}) copy-start(bf16[512,2,3,2,112]{0,4,3,2,1:T(8,128)(2,1)} %slice.147) | copy-start | bytes 4128772
  37.0 4.0 %copy-start.8 = (bf16[512,2,3,1,128]{0,4,3,2,1:T(8,128)(2,1)S(1)}, bf16[512,2,3,1,128]{0,4,3,2,1:T(8,128)(2,1)}, u32[]{:S(2)}) copy-start(bf16[512,2,3,1,128]{0,4,3,2,1:T(8,128)(2,1)} %get-tuple-element.29) | copy-start | bytes 2359300
  60.9 3.1 %copy-start.16 = (f32[3,3,2,128]{3,2,1,0:T(2,128)S(1)}, f32[3,3,2,128]{3,2,1,0:T(2,128)}, u32[]{:S(2)}) copy-start(f32[3,3,2,128]{3,2,1,0:T(2,128)} %get-tuple-element.49) | copy-start | bytes 27652
  60.9 3.1 %copy-start.17 = (f32[3,3,2,128]{3,2,1,0:T(2,128)S(1)}, f32[3,3,2,128]{3,2,1,0:T(2,128)}, u32[]{:S(2)}) copy-start(f32[3,3,2,128]{3,2,1,0:T(2,128)} %get-tuple-element.50) | copy-start | bytes 27652
  75.2 5.7 %copy-start.7 = (bf16[1024,1536]{1,0:T(8,128)(2,1)S(1)}, bf16[1024,1536]{1,0:T(8,128)(2,1)}, u32[]{:S(2)}) copy-start(bf16[1024,1536]{1,0:T(8,128)(2,1)} %pad_maximum_fusion.1) | copy-start | bytes 9437188
  75.2 5.7 %copy-start.11 = (bf16[512,1536,1]{1,0,2:T(8,128)(2,1)S(1)}, bf16[512,1536,1]{1,0,2:T(8,128)(2,1)}, u32[]{:S(2)}) copy-start(bf16[512,1536,1]{1,0,2:T(8,128)(2,1)} %reshape.118) | copy-start | bytes 4718596
  92.6 3.9 %copy-start.9 = (f32[1,2,512,512]{3,2,1,0:T(8,128)S(1)}, f32[1,2,512,512]{3,2,1,0:T(8,128)}, u32[]{:S(2)}) copy-start(f32[1,2,512,512]{3,2,1,0:T(8,128)} %convolution_bitcast_fusion.2) | copy-start | bytes 6291460
  92.7 3.9 %copy-start.10 = (f32[1,2,512,512]{3,2,1,0:T(8,128)S(1)}, f32[1,2,512,512]{3,2,1,0:T(8,128)}, u32[]{:S(2)}) copy-start(f32[1,2,512,512]{3,2,1,0:T(8,128)} %convolution_bitcast_fusion.1) | copy-start | bytes 6291460
  97.8 4.6 %copy-start = (f32[3,2,512,512]{3,2,1,0:T(8,128)}, f32[3,2,512,512]{3,2,1,0:T(8,128)S(1)}, u32[]{:S(2)}) copy-start(f32[3,2,512,512]{3,2,1,0:T(8,128)S(1)} %maximum_multiply_fusion) | copy-start | bytes 18874372
  117.7 6.6 %collective-permute-start.2 = (bf16[2,64,64]{2,1,0:T(8,128)(2,1)S(1)}, bf16[2,64,64]{2,1,0:T(8,128)(2,1)S(1)}, u32[]{:S(2)}, u32[]{:S(2)}) collective-permute-start(bf16[2,64,64]{2,1,0:T(8,128)(2,1)S(1)} %copy-done.12), channel_id=1, source_target_pairs={{0,4},{4,8},{8,12},{12,16},{16,20},{20,24},{24,28},{28,0},{1,5},{5... | collective-permute-start | bytes 49160 | tf_op jit(solution)/shard_map/ppermute | solution.py:18
  124.3 6.6 %collective-permute-start.3 = (bf16[2,64,64]{2,1,0:T(8,128)(2,1)S(1)}, bf16[2,64,64]{2,1,0:T(8,128)(2,1)S(1)}, u32[]{:S(2)}, u32[]{:S(2)}) collective-permute-start(bf16[2,64,64]{2,1,0:T(8,128)(2,1)S(1)} %collective-permute-done.2), channel_id=1, source_target_pairs={{0,4},{4,8},{8,12},{12,16},{16,20},{20,24},{24,28},{28,0},{1,5},{5... | collective-permute-start | bytes 49160 | tf_op jit(solution)/shard_map/ppermute | solution.py:18
  131.0 6.6 %collective-permute-start.4 = (bf16[2,64,64]{2,1,0:T(8,128)(2,1)S(1)}, bf16[2,64,64]{2,1,0:T(8,128)(2,1)S(1)}, u32[]{:S(2)}, u32[]{:S(2)}) collective-permute-start(bf16[2,64,64]{2,1,0:T(8,128)(2,1)S(1)} %collective-permute-done.3), channel_id=1, source_target_pairs={{0,4},{4,8},{8,12},{12,16},{16,20},{20,24},{24,28},{28,0},{1,5},{5... | collective-permute-start | bytes 49160 | tf_op jit(solution)/shard_map/ppermute | solution.py:18
  137.6 6.6 %collective-permute-start.5 = (bf16[2,64,64]{2,1,0:T(8,128)(2,1)S(1)}, bf16[2,64,64]{2,1,0:T(8,128)(2,1)S(1)}, u32[]{:S(2)}, u32[]{:S(2)}) collective-permute-start(bf16[2,64,64]{2,1,0:T(8,128)(2,1)S(1)} %collective-permute-done.4), channel_id=1, source_target_pairs={{0,4},{4,8},{8,12},{12,16},{16,20},{20,24},{24,28},{28,0},{1,5},{5... | collective-permute-start | bytes 49160 | tf_op jit(solution)/shard_map/ppermute | solution.py:18
  144.2 6.7 %collective-permute-start.6 = (bf16[2,64,64]{2,1,0:T(8,128)(2,1)S(1)}, bf16[2,64,64]{2,1,0:T(8,128)(2,1)S(1)}, u32[]{:S(2)}, u32[]{:S(2)}) collective-permute-start(bf16[2,64,64]{2,1,0:T(8,128)(2,1)S(1)} %collective-permute-done.5), channel_id=1, source_target_pairs={{0,4},{4,8},{8,12},{12,16},{16,20},{20,24},{24,28},{28,0},{1,5},{5... | collective-permute-start | bytes 49160 | tf_op jit(solution)/shard_map/ppermute | solution.py:18
  150.9 6.6 %collective-permute-start.7 = (bf16[2,64,64]{2,1,0:T(8,128)(2,1)S(1)}, bf16[2,64,64]{2,1,0:T(8,128)(2,1)S(1)}, u32[]{:S(2)}, u32[]{:S(2)}) collective-permute-start(bf16[2,64,64]{2,1,0:T(8,128)(2,1)S(1)} %collective-permute-done.6), channel_id=1, source_target_pairs={{0,4},{4,8},{8,12},{12,16},{16,20},{20,24},{24,28},{28,0},{1,5},{5... | collective-permute-start | bytes 49160 | tf_op jit(solution)/shard_map/ppermute | solution.py:18
  157.5 6.6 %collective-permute-start.8 = (bf16[2,64,64]{2,1,0:T(8,128)(2,1)S(1)}, bf16[2,64,64]{2,1,0:T(8,128)(2,1)S(1)}, u32[]{:S(2)}, u32[]{:S(2)}) collective-permute-start(bf16[2,64,64]{2,1,0:T(8,128)(2,1)S(1)} %collective-permute-done.7), channel_id=1, source_target_pairs={{0,4},{4,8},{8,12},{12,16},{16,20},{20,24},{24,28},{28,0},{1,5},{5... | collective-permute-start | bytes 49160 | tf_op jit(solution)/shard_map/ppermute | solution.py:18
  (7 other events, 12.6 us)
Sparse Core Ops, SparseCore 0:
  117.1 111.7 reduce-scatter.1
